TPU v7x, 32 devices: a whole 2x2x4 slice. The times are simulated.
32 devices in a mesh: dp: 2 (over y), row: 4 (over x, core), col: 4 (over z).
Axes of the slice: x: 2, y: 2, z: 4, core: 2. Of those that a mesh axis runs over, the one named last changes fastest.
Arguments:
- features: bfloat16 [2, 32, 512, 256], P('dp', 'row', 'col'), may hold values from -6 to 6
- reduce_weight: bfloat16 [256, 128], replicated, may hold values from -0.375 to 0.375
- scale_one: float32 [128], replicated, may hold values from 0.25 to 1.75
- shift_one: float32 [128], replicated, may hold values from -3 to 3
- group_weight: bfloat16 [3, 3, 4, 128], replicated, may hold values from -1 to 1
- scale_two: float32 [128], replicated, may hold values from 0.25 to 1.75
- shift_two: float32 [128], replicated, may hold values from -3 to 3
- expand_weight: bfloat16 [128, 256], replicated, may hold values from -0.5 to 0.5
- scale_three: float32 [256], replicated, may hold values from 0.25 to 1.75
- shift_three: float32 [256], replicated, may hold values from -3 to 3
- cotangent: bfloat16 [2, 32, 512, 256], P('dp', 'row', 'col'), may hold values from -6 to 6
Outputs:
- input_grad: bfloat16 [2, 32, 512, 256], P('dp', 'row', 'col')
- reduce_grad: float32 [256, 128], P('dp')
- group_grad: float32 [128, 3, 3, 4], P('dp')
- expand_grad: float32 [128, 256], P('dp')
All inputs are finite; a program needn't handle non-finite values.
Results may differ from a plain program's by a relative error of at most 0.0069.
Values may be sent and summed in bfloat16 or wider, within the bound.
No kernel may reach another device: no remote copies, remote signals or barrier semaphores. Data moves between devices by JAX's collectives and lax.ppermute only.
A program may use at most 128 MiB of HBM per device.

v0:
```python
import jax
import jax.numpy as jnp
from jax import lax
from jax.sharding import PartitionSpec as P


def extended(block, sides, width):
    for axis, dim in sides:
        count = lax.axis_size(axis)
        forward = [(i, i + 1) for i in range(count - 1)]
        backward = [(target, source) for source, target in forward]
        low = lax.ppermute(
            lax.slice_in_dim(block, block.shape[dim] - width, None, axis=dim), axis, forward
        )
        high = lax.ppermute(lax.slice_in_dim(block, 0, width, axis=dim), axis, backward)
        block = jnp.concatenate([low, block, high], axis=dim)
    return block


def dsilu(value):
    sg = jax.nn.sigmoid(value)
    return sg * (1.0 + value * (1.0 - sg))


def group_conv(inputs, kernel):
    groups = kernel.shape[3] // kernel.shape[2]
    return lax.conv_general_dilated(
        inputs,
        kernel,
        (1, 1),
        ((0, 0), (0, 0)),
        dimension_numbers=("NHWC", "HWIO", "NHWC"),
        feature_group_count=groups,
        preferred_element_type=jnp.float32,
    )


def body(
    features,
    reduce_weight,
    scale_one,
    shift_one,
    group_weight,
    scale_two,
    shift_two,
    expand_weight,
    scale_three,
    shift_three,
    cotangent,
):
    rows = features.shape[1]
    cols = features.shape[2]
    chans = features.shape[3]
    inner = reduce_weight.shape[1]
    group_ch = group_weight.shape[2]
    groups = inner // group_ch
    flat = features.reshape(-1, chans)
    pre_one = (
        jnp.dot(flat, reduce_weight, preferred_element_type=jnp.float32) * scale_one + shift_one
    )
    act_one = jax.nn.silu(pre_one).astype(jnp.bfloat16)
    img_one = act_one.reshape(1, rows, cols, inner)
    padded_act = extended(img_one, (("row", 1), ("col", 2)), 1)
    pre_two = group_conv(padded_act, group_weight).reshape(-1, inner) * scale_two + shift_two
    act_two = jax.nn.silu(pre_two).astype(jnp.bfloat16)
    pre_three = (
        jnp.dot(act_two, expand_weight, preferred_element_type=jnp.float32) * scale_three
        + shift_three
        + flat.astype(jnp.float32)
    )
    back_three = cotangent.reshape(-1, chans).astype(jnp.float32) * dsilu(pre_three)
    grad_three = (back_three * scale_three).astype(jnp.bfloat16)
    gw_three = lax.dot_general(
        act_two, grad_three, (((0,), (0,)), ((), ())), preferred_element_type=jnp.float32
    )
    grad_two = (
        jnp.dot(grad_three, expand_weight.T, preferred_element_type=jnp.float32)
        * dsilu(pre_two)
        * scale_two
    ).astype(jnp.bfloat16)
    padded_grad = extended(grad_two.reshape(1, rows, cols, inner), (("row", 1), ("col", 2)), 1)
    flipped = group_weight[::-1, ::-1].reshape(3, 3, group_ch, groups, group_ch)
    flipped = jnp.transpose(flipped, (0, 1, 4, 3, 2)).reshape(3, 3, group_ch, inner)
    back_one = group_conv(padded_grad, flipped)
    tap_terms = []
    for tap_h in range(3):
        for tap_w in range(3):
            window = padded_act[0, tap_h : tap_h + rows, tap_w : tap_w + cols, :].reshape(-1, inner)
            dense = lax.dot_general(
                window, grad_two, (((0,), (0,)), ((), ())), preferred_element_type=jnp.float32
            )
            blocks = dense.reshape(groups, group_ch, groups, group_ch)
            diag = jnp.diagonal(blocks, axis1=0, axis2=2)
            tap_terms.append(jnp.transpose(diag, (2, 1, 0)).reshape(inner, group_ch))
    gw_two_out = jnp.stack(tap_terms, axis=1).reshape(inner, 3, 3, group_ch)
    grad_one = (back_one.reshape(-1, inner) * dsilu(pre_one) * scale_one).astype(jnp.bfloat16)
    input_grad = (
        jnp.dot(grad_one, reduce_weight.T, preferred_element_type=jnp.float32) + back_three
    ).astype(jnp.bfloat16)
    gw_one = lax.dot_general(
        flat, grad_one, (((0,), (0,)), ((), ())), preferred_element_type=jnp.float32
    )
    summed = lax.psum((gw_one, gw_two_out, gw_three), ("row", "col"))
    shares = (
        lax.psum_scatter(summed[0], "dp", scatter_dimension=0, tiled=True),
        lax.psum_scatter(summed[1], "dp", scatter_dimension=0, tiled=True),
        lax.psum_scatter(summed[2], "dp", scatter_dimension=0, tiled=True),
    )
    total = rows * cols * lax.axis_size("dp") * lax.axis_size("row") * lax.axis_size("col")
    factor = 1.0 / jnp.sqrt(jnp.float32(total))
    return (
        input_grad.reshape(1, rows, cols, chans),
        shares[0] * factor,
        shares[1] * factor,
        shares[2] * factor,
    )


def solution(mesh):
    return jax.shard_map(
        body,
        mesh=mesh,
        in_specs=(
            P("dp", "row", "col", None),
            P(),
            P(),
            P(),
            P(),
            P(),
            P(),
            P(),
            P(),
            P(),
            P("dp", "row", "col", None),
        ),
        out_specs=(
            P("dp", "row", "col", None),
            P("dp", None),
            P("dp", None, None, None),
            P("dp", None),
        ),
        check_vma=False,
    )
```

profile of v0, /device:TPU:8, one launch (start us, length us, event | category | flops | bytes accessed | tf_op | source)
XLA Modules:
  0.0 1005.4 jit_solution(9380093568484053856)
XLA Ops:
  8.0 2.2 multiply_convert_fusion.3
  10.4 1.7 collective-permute-start
  12.1 1.3 collective-permute-start.1
  14.6 1.3 reshape.82
  16.7 3.5 collective-permute-start.2
  20.2 2.4 collective-permute-start.3
  24.8 2.7 collective-permute-done.2
  27.5 3.8 collective-permute-done.3
  31.9 36.1 %copy.89 = bf16[1,10,130,32,4]{4,0,3,2,1:T(2,128)(2,1)} copy(bf16[1,10,130,32,4]{2,4,3,1,0:T(4,128)(2,1)S(1)} %concatenate.46) | data formatting | bytes 665600 | tf_op jit(solution)/shard_map/concatenate | solution.py:16
  68.0 234.4 %convolution_reduce_fusion.1 = f32[8,128,32,4]{3,2,1,0:T(8,128)} fusion(bf16[1,10,130,32,4]{4,0,3,2,1:T(2,128)(2,1)} %copy.89, bf16[3,3,4,32,4]{4,3,2,1,0:T(8,128)(2,1)S(1)} %shard_map.140), kind=kOutput, calls=%fused_computation.10 | convolution fusion | flops 9437184 | bytes 866304 | tf_op jit(solution)/shard_map/conv_general_dilated | solution.py:27
  302.5 14.9 %reshape.158 = f32[1024,128]{1,0:T(8,128)S(1)} reshape(f32[8,128,32,4]{3,2,1,0:T(8,128)} %convolution_reduce_fusion.1) | data formatting | bytes 1048576 | tf_op jit(solution)/shard_map/reshape | solution.py:64
  322.8 1.9 copy.104
  327.6 2.1 convolution_bitcast_fusion.6
  329.7 1.9 copy.110
  335.1 2.1 convolution_bitcast_fusion.5
  337.2 1.9 copy.115
  341.7 1.3 convolution_bitcast_fusion.4
  344.8 2.2 reshape.85
  347.0 3.2 copy.242
  350.2 2.3 gather_fusion.4
  365.1 3.2 collective-permute-start.4
  378.6 3.5 collective-permute-start.6
  382.1 2.4 collective-permute-start.7
  384.5 1.7 fusion.24
  386.3 3.9 collective-permute-done.6
  390.2 3.8 collective-permute-done.7
  394.6 36.1 %copy.96 = bf16[1,10,130,32,4]{4,0,3,2,1:T(2,128)(2,1)} copy(bf16[1,10,130,32,4]{2,4,3,1,0:T(4,128)(2,1)S(1)} %concatenate.49) | data formatting | bytes 665600 | tf_op jit(solution)/shard_map/concatenate | solution.py:16
  430.7 398.5 %convolution_reduce_fusion = f32[8,128,32,4]{3,2,1,0:T(8,128)} fusion(bf16[1,10,130,32,4]{4,0,3,2,1:T(2,128)(2,1)} %copy.96, bf16[3,3,4,32,4]{4,3,2,1,0:T(8,128)(2,1)S(1)} %copy-done.22), kind=kOutput, calls=%fused_computation.9 | convolution fusion | flops 9437184 | bytes 866304 | tf_op jit(solution)/shard_map/conv_general_dilated | solution.py:27
  829.3 14.9 %reshape.159 = f32[1024,128]{1,0:T(8,128)S(1)} reshape(f32[8,128,32,4]{3,2,1,0:T(8,128)} %convolution_reduce_fusion) | data formatting | bytes 1048576 | tf_op jit(solution)/shard_map/reshape | solution.py:96
  847.6 56.6 %psum.25 = f32[64,3,3,4]{0,3,2,1:T(4,128)S(1)} all-reduce(f32[64,3,3,4]{0,3,2,1:T(4,128)S(1)} %copy.175), channel_id=1, replica_groups=mesh['dp'=2,'row'=4,'col'=4] {'row','col'}, use_global_device_ids=true, to_apply=%region_2.3 | all-reduce | flops 2304 | bytes 18432 | tf_op jit(solution)/shard_map/psum | solution.py:103
  904.9 90.5 %all-reduce.3.cloned.1.call-done = (f32[128,128]{0,1:T(8,128)}, f32[64,256]{1,0:T(8,128)}) async-done(((f32[128,128]{0,1:T(8,128)}, f32[64,256]{1,0:T(8,128)}), (f32[128,128]{0,1:T(8,128)}, f32[64,256]{1,0:T(8,128)})) %all-reduce.3.cloned.1.call-update) | async-done | bytes 131088 | tf_op jit(solution)/shard_map/psum | solution.py:103
  996.9 1.5 broadcast_multiply_fusion
  (186 shorter events, 50.8 us)
Async XLA Ops:
  7.2 6.8 copy-start.26
  7.2 839.3 %reduce-scatter.10.cloned.1.call-start = ((), (), s32[]{:S(2)}) async-start(), calls=%async_computation.5 | async-start | bytes 98304
  10.2 12.7 %copy-start.4 = (bf16[1024,128]{1,0:T(8,128)(2,1)}, bf16[1024,128]{1,0:T(8,128)(2,1)S(1)}, u32[]{:S(2)}) copy-start(bf16[1024,128]{1,0:T(8,128)(2,1)S(1)} %get-tuple-element.36) | copy-start | bytes 786436
  10.4 20.9 %copy-start.2 = (bf16[1,8,128,128]{2,3,1,0:T(8,128)(2,1)}, bf16[1,8,128,128]{2,3,1,0:T(8,128)(2,1)S(1)}, u32[]{:S(2)}) copy-start(bf16[1,8,128,128]{2,3,1,0:T(8,128)(2,1)S(1)} %copy.86) | copy-start | bytes 786436
  10.4 5.5 collective-permute-start
  12.1 4.4 collective-permute-start.1
  15.9 15.3 %copy-start.13 = (bf16[1,1,128,128]{2,3,1,0:T(8,128)(2,1)}, bf16[1,1,128,128]{2,3,1,0:T(8,128)(2,1)S(1)}, u32[]{:S(2)}) copy-start(bf16[1,1,128,128]{2,3,1,0:T(8,128)(2,1)S(1)} %collective-permute-done) | copy-start | bytes 98308
  16.5 14.8 %copy-start.15 = (bf16[1,1,128,128]{2,3,1,0:T(8,128)(2,1)}, bf16[1,1,128,128]{2,3,1,0:T(8,128)(2,1)S(1)}, u32[]{:S(2)}) copy-start(bf16[1,1,128,128]{2,3,1,0:T(8,128)(2,1)S(1)} %collective-permute-done.1) | copy-start | bytes 98308
  16.7 10.8 %collective-permute-start.2 = (bf16[1,10,1,128]{2,3,1,0:T(8,128)(2,1)S(1)}, bf16[1,10,1,128]{2,3,1,0:T(8,128)(2,1)S(1)}, u32[]{:S(2)}, u32[]{:S(2)}) collective-permute-start(bf16[1,10,1,128]{2,3,1,0:T(8,128)(2,1)S(1)} %get-tuple-element.28), channel_id=1, source_target_pairs={{0,1},{1,2},{2,3},{4,5},{5,6},{6,7},{8,9},{9,10},{10,11},{12,13},{... | collective-permute-start | bytes 7688 | tf_op jit(solution)/shard_map/ppermute | solution.py:12
  20.2 11.0 %collective-permute-start.3 = (bf16[1,10,1,128]{2,3,1,0:T(8,128)(2,1)S(1)}, bf16[1,10,1,128]{2,3,1,0:T(8,128)(2,1)S(1)}, u32[]{:S(2)}, u32[]{:S(2)}) collective-permute-start(bf16[1,10,1,128]{2,3,1,0:T(8,128)(2,1)S(1)} %get-tuple-element.29), channel_id=1, source_target_pairs={{1,0},{2,1},{3,2},{5,4},{6,5},{7,6},{9,8},{10,9},{11,10},{13,12},{... | collective-permute-start | bytes 7688 | tf_op jit(solution)/shard_map/ppermute | solution.py:15
  27.5 40.5 %copy-start.6 = (bf16[1,10,1,128]{2,3,1,0:T(8,128)(2,1)}, bf16[1,10,1,128]{2,3,1,0:T(8,128)(2,1)S(1)}, u32[]{:S(2)}) copy-start(bf16[1,10,1,128]{2,3,1,0:T(8,128)(2,1)S(1)} %collective-permute-done.2) | copy-start | bytes 7684
  31.3 36.7 %copy-start.8 = (bf16[1,10,1,128]{2,3,1,0:T(8,128)(2,1)}, bf16[1,10,1,128]{2,3,1,0:T(8,128)(2,1)S(1)}, u32[]{:S(2)}) copy-start(bf16[1,10,1,128]{2,3,1,0:T(8,128)(2,1)S(1)} %collective-permute-done.3) | copy-start | bytes 7684
  302.4 14.9 %copy-start.20 = (bf16[1,8,128,256]{3,2,1,0:T(8,128)(2,1)S(1)}, bf16[1,8,128,256]{3,2,1,0:T(8,128)(2,1)}, u32[]{:S(2)}) copy-start(bf16[1,8,128,256]{3,2,1,0:T(8,128)(2,1)} %param.11) | copy-start | bytes 1572868
  302.4 14.9 %copy-start.28 = (bf16[1,8,128,256]{3,2,1,0:T(8,128)(2,1)S(1)}, bf16[1,8,128,256]{3,2,1,0:T(8,128)(2,1)}, u32[]{:S(2)}) copy-start(bf16[1,8,128,256]{3,2,1,0:T(8,128)(2,1)} %param.21) | copy-start | bytes 1572868
  302.4 14.9 %copy-start.29 = (bf16[128,256]{1,0:T(8,128)(2,1)S(1)}, bf16[128,256]{1,0:T(8,128)(2,1)}, u32[]{:S(2)}) copy-start(bf16[128,256]{1,0:T(8,128)(2,1)} %param.18) | copy-start | bytes 196612
  302.4 14.9 %copy-start.30 = (f32[256]{0:T(256)S(1)}, f32[256]{0:T(256)}, u32[]{:S(2)}) copy-start(f32[256]{0:T(256)} %param.20) | copy-start | bytes 3076
  302.4 15.0 %copy-start.31 = (f32[256]{0:T(256)S(1)}, f32[256]{0:T(256)}, u32[]{:S(2)}) copy-start(f32[256]{0:T(256)} %param.19) | copy-start | bytes 3076
  302.4 15.0 %copy-start.32 = (f32[128]{0:T(128)S(1)}, f32[128]{0:T(128)}, u32[]{:S(2)}) copy-start(f32[128]{0:T(128)} %param.17) | copy-start | bytes 1540
  302.5 15.0 %copy-start.33 = (f32[128]{0:T(128)S(1)}, f32[128]{0:T(128)}, u32[]{:S(2)}) copy-start(f32[128]{0:T(128)} %param.16) | copy-start | bytes 1540
  364.1 20.4 %copy-start.11 = (f32[1024,256]{1,0:T(8,128)S(1)}, f32[1024,256]{1,0:T(8,128)}, u32[]{:S(2)}) copy-start(f32[1024,256]{1,0:T(8,128)} %copy-done.10) | copy-start | bytes 3145732
  364.8 19.8 %copy-start.19 = (f32[1024,128]{1,0:T(8,128)S(1)}, f32[1024,128]{1,0:T(8,128)}, u32[]{:S(2)}) copy-start(f32[1024,128]{1,0:T(8,128)} %copy-done.18) | copy-start | bytes 1572868
  365.1 13.3 %collective-permute-start.4 = (bf16[1,1,128,128]{2,3,1,0:T(8,128)(2,1)S(1)}, bf16[1,1,128,128]{2,3,1,0:T(8,128)(2,1)S(1)}, u32[]{:S(2)}, u32[]{:S(2)}) collective-permute-start(bf16[1,1,128,128]{2,3,1,0:T(8,128)(2,1)S(1)} %get-tuple-element.32), channel_id=1, source_target_pairs={{0,4},{4,8},{8,12},{1,5},{5,9},{9,13},{2,6},{6,10},{10,14},{3,7},{... | collective-permute-start | bytes 98312 | tf_op jit(solution)/shard_map/ppermute | solution.py:12
  368.3 10.1 %collective-permute-start.5 = (bf16[1,1,128,128]{2,3,1,0:T(8,128)(2,1)S(1)}, bf16[1,1,128,128]{2,3,1,0:T(8,128)(2,1)S(1)}, u32[]{:S(2)}, u32[]{:S(2)}) collective-permute-start(bf16[1,1,128,128]{2,3,1,0:T(8,128)(2,1)S(1)} %get-tuple-element.33), channel_id=1, source_target_pairs={{4,0},{8,4},{12,8},{5,1},{9,5},{13,9},{6,2},{10,6},{14,10},{7,3},{... | collective-permute-start | bytes 98312 | tf_op jit(solution)/shard_map/ppermute | solution.py:15
  378.3 525.9 %reduce-scatter.8.cloned.1.call-start = ((), (), s32[]{:S(2)}) async-start(), calls=%async_computation.4 | async-start | bytes 196608 | tf_op jit(solution)/shard_map/reduce_scatter | solution.py:107
  378.6 11.5 %collective-permute-start.6 = (bf16[1,10,1,128]{2,3,1,0:T(8,128)(2,1)S(1)}, bf16[1,10,1,128]{2,3,1,0:T(8,128)(2,1)S(1)}, u32[]{:S(2)}, u32[]{:S(2)}) collective-permute-start(bf16[1,10,1,128]{2,3,1,0:T(8,128)(2,1)S(1)} %get-tuple-element.26), channel_id=1, source_target_pairs={{0,1},{1,2},{2,3},{4,5},{5,6},{6,7},{8,9},{9,10},{10,11},{12,13},{... | collective-permute-start | bytes 7688 | tf_op jit(solution)/shard_map/ppermute | solution.py:12
  382.1 11.9 %collective-permute-start.7 = (bf16[1,10,1,128]{2,3,1,0:T(8,128)(2,1)S(1)}, bf16[1,10,1,128]{2,3,1,0:T(8,128)(2,1)S(1)}, u32[]{:S(2)}, u32[]{:S(2)}) collective-permute-start(bf16[1,10,1,128]{2,3,1,0:T(8,128)(2,1)S(1)} %get-tuple-element.27), channel_id=1, source_target_pairs={{1,0},{2,1},{3,2},{5,4},{6,5},{7,6},{9,8},{10,9},{11,10},{13,12},{... | collective-permute-start | bytes 7688 | tf_op jit(solution)/shard_map/ppermute | solution.py:15
  386.3 518.0 %reduce-scatter.6.cloned.1.call-start = ((), (), s32[]{:S(2)}) async-start(), calls=%async_computation.3 | async-start | bytes 196608 | tf_op jit(solution)/shard_map/reduce_scatter | solution.py:105
  394.6 36.1 %copy-start.22 = (bf16[3,3,4,32,4]{4,3,2,1,0:T(8,128)(2,1)S(1)}, bf16[3,3,4,32,4]{4,3,2,1,0:T(8,128)(2,1)}, u32[]{:S(2)}) copy-start(bf16[3,3,4,32,4]{4,3,2,1,0:T(8,128)(2,1)} %reshape.82) | copy-start | bytes 27652
  829.2 14.9 %copy-start.17 = (f32[1024,128]{1,0:T(8,128)S(1)}, f32[1024,128]{1,0:T(8,128)}, u32[]{:S(2)}) copy-start(f32[1024,128]{1,0:T(8,128)} %get-tuple-element.37) | copy-start | bytes 1572868
  829.3 14.9 %copy-start.27 = (f32[128]{0:T(128)S(1)}, f32[128]{0:T(128)}, u32[]{:S(2)}) copy-start(f32[128]{0:T(128)} %param.13) | copy-start | bytes 1540
  829.3 15.1 %copy-start.21 = (bf16[1,8,128,256]{3,2,1,0:T(8,128)(2,1)S(1)}, bf16[1,8,128,256]{3,2,1,0:T(8,128)(2,1)}, u32[]{:S(2)}) copy-start(bf16[1,8,128,256]{3,2,1,0:T(8,128)(2,1)} %param.11) | copy-start | bytes 1572868
  845.3 150.0 %all-reduce.3.cloned.1.call-start = ((), (), s32[]{:S(2)}) async-start(), calls=%async_computation.6 | async-start | bytes 262144 | tf_op jit(solution)/shard_map/psum | solution.py:103
  (14 other events, 28.2 us)
Sparse Core Ops, SparseCore 0:
  378.5 12.0 reduce-scatter.9
  392.8 10.2 reduce-scatter.7
  845.4 9.5 reduce-scatter.5
  904.4 90.9 all-reduce.2
where the time goes:
time: 1010 us
  matrix products  648 us (64%)
  local copies, waits for them, and re-layouts  156 us (15%)
  waiting for transfers between devices  105 us (10%)
  blocking collectives  56.6 us (6%)
  starting transfers between devices  19.4 us (2%)
  between operations  15.1 us (1%)
    conv_general_dilated x2, matrix products, group_conv(): lax.conv_general_dilated(inputs, kernel, (1, 1), ((0, 0), (0, 0)), dimens...  633 us
    psum x1, waiting for transfers between devices, body(): summed = lax.psum((gw_one, gw_two_out, gw_three), ('row', 'col'))  90.5 us
    concatenate x4, local copies, waits for them, and re-layouts, extended(): block = jnp.concatenate([low, block, high], axis=dim)  72.6 us
    psum x1, blocking collectives, body(): summed = lax.psum((gw_one, gw_two_out, gw_three), ('row', 'col'))  56.6 us
  transfers between devices with their start and end apart: 12, of which 6 were waited for; matrix products, arithmetic and copies ran while one was open for 47% of the time, Pallas kernels for 0%

commit v1 on v0

--- a/solution.py
+++ b/solution.py
@@ -100,7 +100,7 @@
     gw_one = lax.dot_general(
         flat, grad_one, (((0,), (0,)), ((), ())), preferred_element_type=jnp.float32
     )
-    summed = lax.psum((gw_one, gw_two_out, gw_three), ("row", "col"))
+    summed = lax.psum(lax.psum((gw_one, gw_two_out, gw_three), "col"), "row")
     shares = (
         lax.psum_scatter(summed[0], "dp", scatter_dimension=0, tiled=True),
         lax.psum_scatter(summed[1], "dp", scatter_dimension=0, tiled=True),

time: 1010 us -> 944 us (0.935)
  waiting for transfers between devices: 105 us -> 69.3 us
  blocking collectives: 56.6 us -> 25.6 us
    psum x1 -> x2, waiting for transfers between devices: 90.5 us -> 43.1 us  [body(): summed = lax.psum(lax.psum((gw_one, gw_two_out, gw_three), 'col'), 'row')]
    psum x1 -> x2, blocking collectives: 56.6 us -> 25.6 us  [body(): summed = lax.psum(lax.psum((gw_one, gw_two_out, gw_three), 'col'), 'row')]
    unnamed x5 -> x6, waiting for transfers between devices: 0.07 us -> 11.6 us
  transfers between devices with their start and end apart: 12 -> 13, of which waited for: 6 -> 9; matrix products, arithmetic and copies ran while one was open for 47% -> 51% of each run, Pallas kernels for 0% -> 0%
where the time goes in v1:
time: 944 us; the launch traced here: 938 us
  matrix products  650 us (69%)
  local copies, waits for them, and re-layouts  153 us (16%)
  waiting for transfers between devices  69.3 us (7%)
  blocking collectives  25.6 us (3%)
  starting transfers between devices  19.4 us (2%)
  between operations  14.8 us (2%)
    conv_general_dilated x2, matrix products, group_conv(): lax.conv_general_dilated(inputs, kernel, (1, 1), ((0, 0), (0, 0)), dimens...  633 us
    concatenate x4, local copies, waits for them, and re-layouts, extended(): block = jnp.concatenate([low, block, high], axis=dim)  72.6 us
    psum x2, waiting for transfers between devices, body(): summed = lax.psum(lax.psum((gw_one, gw_two_out, gw_three), 'col'), 'row')  43.1 us
    psum x2, blocking collectives, body(): summed = lax.psum(lax.psum((gw_one, gw_two_out, gw_three), 'col'), 'row')  25.6 us
  transfers between devices with their start and end apart: 13, of which 9 were waited for; matrix products, arithmetic and copies ran while one was open for 51% of the time, Pallas kernels for 0%

profile of v1, /device:TPU:8, one launch (start us, length us, event | category | flops | bytes accessed | tf_op | source)
XLA Modules:
  0.0 938.1 jit_solution(8892262451598347505)
XLA Ops:
  8.0 2.1 multiply_convert_fusion.3
  10.4 1.7 collective-permute-start
  16.7 3.5 collective-permute-start.2
  20.2 2.4 collective-permute-start.3
  24.8 2.7 collective-permute-done.2
  27.5 3.8 collective-permute-done.3
  31.9 36.1 %copy.89 = bf16[1,10,130,32,4]{4,0,3,2,1:T(2,128)(2,1)} copy(bf16[1,10,130,32,4]{2,4,3,1,0:T(4,128)(2,1)S(1)} %concatenate.46) | data formatting | bytes 665600 | tf_op jit(solution)/shard_map/concatenate | solution.py:16
  68.0 234.5 %convolution_reduce_fusion.1 = f32[8,128,32,4]{3,2,1,0:T(8,128)} fusion(bf16[1,10,130,32,4]{4,0,3,2,1:T(2,128)(2,1)} %copy.89, bf16[3,3,4,32,4]{4,3,2,1,0:T(8,128)(2,1)S(1)} %shard_map.140), kind=kOutput, calls=%fused_computation.10 | convolution fusion | flops 9437184 | bytes 866304 | tf_op jit(solution)/shard_map/conv_general_dilated | solution.py:27
  302.6 14.9 %reshape.158 = f32[1024,128]{1,0:T(8,128)S(1)} reshape(f32[8,128,32,4]{3,2,1,0:T(8,128)} %convolution_reduce_fusion.1) | data formatting | bytes 1048576 | tf_op jit(solution)/shard_map/reshape | solution.py:64
  323.8 1.9 copy.104
  328.5 2.1 convolution_bitcast_fusion.6
  330.6 1.9 copy.110
  336.0 2.1 convolution_bitcast_fusion.5
  338.1 1.9 copy.115
  345.9 2.2 reshape.85
  348.1 3.2 copy.242
  351.3 2.3 gather_fusion.4
  358.6 3.2 collective-permute-start.4
  367.4 3.5 collective-permute-start.6
  370.9 2.4 collective-permute-start.7
  373.9 1.9 copy.132
  378.9 3.9 collective-permute-done.7
  384.4 36.1 %copy.96 = bf16[1,10,130,32,4]{4,0,3,2,1:T(2,128)(2,1)} copy(bf16[1,10,130,32,4]{2,4,3,1,0:T(4,128)(2,1)S(1)} %concatenate.49) | data formatting | bytes 665600 | tf_op jit(solution)/shard_map/concatenate | solution.py:16
  420.5 398.6 %convolution_reduce_fusion = f32[8,128,32,4]{3,2,1,0:T(8,128)} fusion(bf16[1,10,130,32,4]{4,0,3,2,1:T(2,128)(2,1)} %copy.96, bf16[3,3,4,32,4]{4,3,2,1,0:T(8,128)(2,1)S(1)} %copy-done.20), kind=kOutput, calls=%fused_computation.9 | convolution fusion | flops 9437184 | bytes 866304 | tf_op jit(solution)/shard_map/conv_general_dilated | solution.py:27
  819.1 14.9 %reshape.159 = f32[1024,128]{1,0:T(8,128)S(1)} reshape(f32[8,128,32,4]{3,2,1,0:T(8,128)} %convolution_reduce_fusion) | data formatting | bytes 1048576 | tf_op jit(solution)/shard_map/reshape | solution.py:96
  837.7 1.9 copy.143
  843.1 2.0 reduce-scatter.6.cloned.1.call-done
  846.3 11.5 %reduce-scatter.10.cloned.1.call-done = f32[64,36]{1,0:T(8,128)} async-done(((f32[128,36]{1,0:T(8,128)}), f32[64,36]{1,0:T(8,128)}) %reduce-scatter.10.cloned.1.call-update) | async-done | bytes 9232
  858.9 15.4 %psum.52 = f32[64,3,3,4]{0,3,2,1:T(4,128)S(1)} all-reduce(f32[64,3,3,4]{0,3,2,1:T(4,128)S(1)} %copy.175), channel_id=1, replica_groups=mesh['dp'=2,'row'=4,'col'=4] {'col'}, use_global_device_ids=true, to_apply=%region_3.4 | all-reduce | flops 2304 | bytes 18432 | tf_op jit(solution)/shard_map/psum | solution.py:103
  874.3 10.2 %psum.49 = f32[64,3,3,4]{0,3,2,1:T(4,128)S(1)} all-reduce(f32[64,3,3,4]{0,3,2,1:T(4,128)S(1)} %psum.52), channel_id=1, replica_groups=mesh['dp'=2,'row'=4,'col'=4] {'row'}, use_global_device_ids=true, to_apply=%region_4.5 | all-reduce | flops 2304 | bytes 18432 | tf_op jit(solution)/shard_map/psum | solution.py:103
  884.5 10.1 %all-reduce.5.cloned.1.call-done = (f32[128,128]{0,1:T(8,128)}, f32[64,256]{1,0:T(8,128)}) async-done(((f32[128,128]{0,1:T(8,128)}, f32[64,256]{1,0:T(8,128)}), (f32[128,128]{0,1:T(8,128)}, f32[64,256]{1,0:T(8,128)})) %all-reduce.5.cloned.1.call-update) | async-done | bytes 131088 | tf_op jit(solution)/shard_map/psum | solution.py:103
  895.2 33.1 %all-reduce.7.cloned.1.call-done = (f32[128,128]{0,1:T(8,128)}, f32[64,256]{1,0:T(8,128)}) async-done(((f32[128,128]{0,1:T(8,128)}, f32[64,256]{1,0:T(8,128)}), (f32[128,128]{0,1:T(8,128)}, f32[64,256]{1,0:T(8,128)})) %all-reduce.7.cloned.1.call-update) | async-done | bytes 131088 | tf_op jit(solution)/shard_map/psum | solution.py:103
  (190 shorter events, 55.5 us)
Async XLA Ops:
  7.2 6.8 copy-start.25
  7.2 835.9 %reduce-scatter.8.cloned.1.call-start = ((), (), s32[]{:S(2)}) async-start(), calls=%async_computation.4 | async-start | bytes 196608 | tf_op jit(solution)/shard_map/reduce_scatter | solution.py:107
  10.2 12.7 %copy-start.5 = (bf16[1024,128]{1,0:T(8,128)(2,1)}, bf16[1024,128]{1,0:T(8,128)(2,1)S(1)}, u32[]{:S(2)}) copy-start(bf16[1024,128]{1,0:T(8,128)(2,1)S(1)} %get-tuple-element.38) | copy-start | bytes 786436
  10.3 20.9 %copy-start.3 = (bf16[1,8,128,128]{2,3,1,0:T(8,128)(2,1)}, bf16[1,8,128,128]{2,3,1,0:T(8,128)(2,1)S(1)}, u32[]{:S(2)}) copy-start(bf16[1,8,128,128]{2,3,1,0:T(8,128)(2,1)S(1)} %copy.86) | copy-start | bytes 786436
  10.4 5.6 collective-permute-start
  12.1 4.4 collective-permute-start.1
  16.0 15.3 %copy-start.13 = (bf16[1,1,128,128]{2,3,1,0:T(8,128)(2,1)}, bf16[1,1,128,128]{2,3,1,0:T(8,128)(2,1)S(1)}, u32[]{:S(2)}) copy-start(bf16[1,1,128,128]{2,3,1,0:T(8,128)(2,1)S(1)} %collective-permute-done) | copy-start | bytes 98308
  16.5 14.8 %copy-start.15 = (bf16[1,1,128,128]{2,3,1,0:T(8,128)(2,1)}, bf16[1,1,128,128]{2,3,1,0:T(8,128)(2,1)S(1)}, u32[]{:S(2)}) copy-start(bf16[1,1,128,128]{2,3,1,0:T(8,128)(2,1)S(1)} %collective-permute-done.1) | copy-start | bytes 98308
  16.7 10.8 %collective-permute-start.2 = (bf16[1,10,1,128]{2,3,1,0:T(8,128)(2,1)S(1)}, bf16[1,10,1,128]{2,3,1,0:T(8,128)(2,1)S(1)}, u32[]{:S(2)}, u32[]{:S(2)}) collective-permute-start(bf16[1,10,1,128]{2,3,1,0:T(8,128)(2,1)S(1)} %get-tuple-element.30), channel_id=1, source_target_pairs={{0,1},{1,2},{2,3},{4,5},{5,6},{6,7},{8,9},{9,10},{10,11},{12,13},{... | collective-permute-start | bytes 7688 | tf_op jit(solution)/shard_map/ppermute | solution.py:12
  20.2 11.0 %collective-permute-start.3 = (bf16[1,10,1,128]{2,3,1,0:T(8,128)(2,1)S(1)}, bf16[1,10,1,128]{2,3,1,0:T(8,128)(2,1)S(1)}, u32[]{:S(2)}, u32[]{:S(2)}) collective-permute-start(bf16[1,10,1,128]{2,3,1,0:T(8,128)(2,1)S(1)} %get-tuple-element.31), channel_id=1, source_target_pairs={{1,0},{2,1},{3,2},{5,4},{6,5},{7,6},{9,8},{10,9},{11,10},{13,12},{... | collective-permute-start | bytes 7688 | tf_op jit(solution)/shard_map/ppermute | solution.py:15
  27.5 40.5 %copy-start.7 = (bf16[1,10,1,128]{2,3,1,0:T(8,128)(2,1)}, bf16[1,10,1,128]{2,3,1,0:T(8,128)(2,1)S(1)}, u32[]{:S(2)}) copy-start(bf16[1,10,1,128]{2,3,1,0:T(8,128)(2,1)S(1)} %collective-permute-done.2) | copy-start | bytes 7684
  31.3 36.7 %copy-start.9 = (bf16[1,10,1,128]{2,3,1,0:T(8,128)(2,1)}, bf16[1,10,1,128]{2,3,1,0:T(8,128)(2,1)S(1)}, u32[]{:S(2)}) copy-start(bf16[1,10,1,128]{2,3,1,0:T(8,128)(2,1)S(1)} %collective-permute-done.3) | copy-start | bytes 7684
  302.6 14.9 %copy-start.18 = (bf16[1,8,128,256]{3,2,1,0:T(8,128)(2,1)S(1)}, bf16[1,8,128,256]{3,2,1,0:T(8,128)(2,1)}, u32[]{:S(2)}) copy-start(bf16[1,8,128,256]{3,2,1,0:T(8,128)(2,1)} %param.11) | copy-start | bytes 1572868
  302.6 14.9 %copy-start.28 = (bf16[1,8,128,256]{3,2,1,0:T(8,128)(2,1)S(1)}, bf16[1,8,128,256]{3,2,1,0:T(8,128)(2,1)}, u32[]{:S(2)}) copy-start(bf16[1,8,128,256]{3,2,1,0:T(8,128)(2,1)} %param.21) | copy-start | bytes 1572868
  302.6 14.9 %copy-start.29 = (bf16[128,256]{1,0:T(8,128)(2,1)S(1)}, bf16[128,256]{1,0:T(8,128)(2,1)}, u32[]{:S(2)}) copy-start(bf16[128,256]{1,0:T(8,128)(2,1)} %param.18) | copy-start | bytes 196612
  302.6 14.9 %copy-start.30 = (f32[256]{0:T(256)S(1)}, f32[256]{0:T(256)}, u32[]{:S(2)}) copy-start(f32[256]{0:T(256)} %param.20) | copy-start | bytes 3076
  302.6 14.9 %copy-start.31 = (f32[256]{0:T(256)S(1)}, f32[256]{0:T(256)}, u32[]{:S(2)}) copy-start(f32[256]{0:T(256)} %param.19) | copy-start | bytes 3076
  302.6 14.9 %copy-start.32 = (f32[128]{0:T(128)S(1)}, f32[128]{0:T(128)}, u32[]{:S(2)}) copy-start(f32[128]{0:T(128)} %param.17) | copy-start | bytes 1540
  302.6 14.9 %copy-start.33 = (f32[128]{0:T(128)S(1)}, f32[128]{0:T(128)}, u32[]{:S(2)}) copy-start(f32[128]{0:T(128)} %param.16) | copy-start | bytes 1540
  358.6 8.6 collective-permute-start.4
  361.7 5.4 collective-permute-start.5
  367.4 11.5 %collective-permute-start.6 = (bf16[1,10,1,128]{2,3,1,0:T(8,128)(2,1)S(1)}, bf16[1,10,1,128]{2,3,1,0:T(8,128)(2,1)S(1)}, u32[]{:S(2)}, u32[]{:S(2)}) collective-permute-start(bf16[1,10,1,128]{2,3,1,0:T(8,128)(2,1)S(1)} %get-tuple-element.28), channel_id=1, source_target_pairs={{0,1},{1,2},{2,3},{4,5},{5,6},{6,7},{8,9},{9,10},{10,11},{12,13},{... | collective-permute-start | bytes 7688 | tf_op jit(solution)/shard_map/ppermute | solution.py:12
  370.9 11.9 %collective-permute-start.7 = (bf16[1,10,1,128]{2,3,1,0:T(8,128)(2,1)S(1)}, bf16[1,10,1,128]{2,3,1,0:T(8,128)(2,1)}, u32[]{:S(2)}, u32[]{:S(2)}) collective-permute-start(bf16[1,10,1,128]{2,3,1,0:T(8,128)(2,1)S(1)} %get-tuple-element.29), channel_id=1, source_target_pairs={{1,0},{2,1},{3,2},{5,4},{6,5},{7,6},{9,8},{10,9},{11,10},{13,12},{... | collective-permute-start | bytes 7688 | tf_op jit(solution)/shard_map/ppermute | solution.py:15
  377.2 467.9 %reduce-scatter.6.cloned.1.call-start = ((), (), s32[]{:S(2)}) async-start(), calls=%async_computation.3 | async-start | bytes 196608 | tf_op jit(solution)/shard_map/reduce_scatter | solution.py:105
  384.3 36.1 %copy-start.20 = (bf16[3,3,4,32,4]{4,3,2,1,0:T(8,128)(2,1)S(1)}, bf16[3,3,4,32,4]{4,3,2,1,0:T(8,128)(2,1)}, u32[]{:S(2)}) copy-start(bf16[3,3,4,32,4]{4,3,2,1,0:T(8,128)(2,1)} %reshape.82) | copy-start | bytes 27652
  819.1 14.9 %copy-start.17 = (f32[1024,128]{1,0:T(8,128)S(1)}, f32[1024,128]{1,0:T(8,128)}, u32[]{:S(2)}) copy-start(f32[1024,128]{1,0:T(8,128)} %get-tuple-element.39) | copy-start | bytes 1572868
  819.1 14.9 %copy-start.27 = (f32[128]{0:T(128)S(1)}, f32[128]{0:T(128)}, u32[]{:S(2)}) copy-start(f32[128]{0:T(128)} %param.13) | copy-start | bytes 1540
  819.1 15.1 %copy-start.19 = (bf16[1,8,128,256]{3,2,1,0:T(8,128)(2,1)S(1)}, bf16[1,8,128,256]{3,2,1,0:T(8,128)(2,1)}, u32[]{:S(2)}) copy-start(bf16[1,8,128,256]{3,2,1,0:T(8,128)(2,1)} %param.11) | copy-start | bytes 1572868
  835.2 22.6 %reduce-scatter.10.cloned.1.call-start = ((), (), s32[]{:S(2)}) async-start(), calls=%async_computation.5 | async-start | bytes 98304
  836.9 8.3 copy-start.12
  843.0 51.5 %all-reduce.5.cloned.1.call-start = ((), (), s32[]{:S(2)}) async-start(), calls=%async_computation.6 | async-start | bytes 262144 | tf_op jit(solution)/shard_map/psum | solution.py:103
  845.1 83.2 %all-reduce.7.cloned.1.call-start = ((), (), s32[]{:S(2)}) async-start(), calls=%async_computation.7 | async-start | bytes 262144 | tf_op jit(solution)/shard_map/psum | solution.py:103
  (15 other events, 29.9 us)
Sparse Core Ops, SparseCore 0:
  377.3 12.7 reduce-scatter.7
  835.3 9.7 reduce-scatter.5
  847.9 9.8 reduce-scatter.9
  860.0 34.5 all-reduce.4
  896.9 31.3 all-reduce.6
